TPU v7x, 32 devices: a whole 2x2x4 slice. The times are simulated.
32 devices in a mesh: row: 4 (over x, core), col: 8 (over z, y).
Axes of the slice: x: 2, y: 2, z: 4, core: 2. Of those that a mesh axis runs over, the one named last changes fastest.
Arguments:
- schur: float32 [4096, 4096], P('row', 'col'), may hold values from -6 to 6
- left_rot: float32 [8, 512, 512], P('row', 'col'), may hold values from -1 to 1, as said below
- right_rot: float32 [8, 512, 512], P('col', 'row'), may hold values from -1 to 1, as said below
- left_off: float32 [8, 512, 512], P('row', 'col'), may hold values from -1 to 1, as said below
- right_off: float32 [8, 512, 512], P('col', 'row'), may hold values from -1 to 1, as said below
Outputs:
- updated: float32 [4096, 4096], P('row', 'col')
Inputs may be any that keep to these rules, and one draw needn't show every extreme that they name: `left_rot`: each 512 x 512 block is orthogonal. `right_rot`: each 512 x 512 block is orthogonal. `left_off`: each 512 x 512 block is orthogonal. `right_off`: each 512 x 512 block is orthogonal.
All inputs are finite; a program needn't handle non-finite values.
Results may differ from a plain program's by a relative error of at most 0.00007.
Values sent between devices are 32-bit elements; how exact they have to be, the bound alone decides.
A program may use at most 64 MiB of HBM per device.

v0:
```python
import functools

import jax
import jax.numpy as jnp
from jax import lax
from jax.experimental import pallas as pl
from jax.experimental.pallas import tpu as pltpu
from jax.sharding import PartitionSpec as P

MESH = pl.DeviceIdType.MESH
F32 = jnp.float32
BF16 = jnp.bfloat16


def run(pred, fn):
    if pred is None:
        fn()
    else:
        pl.when(pred)(fn)


def both(a, b):
    if a is None:
        return b
    if b is None:
        return a
    return jnp.logical_and(a, b)


def split(v):
    high = v.astype(BF16)
    return high, (v - high.astype(F32)).astype(BF16)


def dot3(a, b, dims):
    def one(p, q):
        return lax.dot_general(p, q, (dims, ((), ())), preferred_element_type=F32)

    return one(a[0], b[0]) + (one(a[0], b[1]) + one(a[1], b[0]))


RIGHT = ((1,), (0,))
LEFT = ((0,), (0,))


def kernel(
    R, C, chunk,
    x_in, rr_in, ro_in, lr_in, lo_in, out,
    x, rr, ro, nx, lr, lo, nl, m, m2, m3, hp, hn, ha, hb,
    rr_h, rr_l, ro_h, ro_l, nx_h, nx_l,
    rr_s, rr_r, ro_s, ro_r, nx_s, nx_r, lr_s, lr_r, lo_s, lo_r, nl_s, nl_r,
    hp_s, hp_r, hn_s, hn_r, hr_s, hr_r, x_s,
):
    r = lax.axis_index("row")
    c = lax.axis_index("col")
    L = C // 2
    line = lax.div(c, 2)
    y = lax.rem(c, 2)
    mate = 2 * line + 1 - y
    c_next, c_prev = lax.rem(c + 1, C), lax.rem(c + C - 1, C)
    r_next, r_prev = lax.rem(r + 1, R), lax.rem(r + R - 1, R)
    can_up, can_down = line < L - 1, line > 0
    c_up, c_down = lax.rem(c + 2, C), lax.rem(c + C - 2, C)
    rows, cols = x.shape
    win = lr_in.shape[2]
    half = win // 2
    nr = rr_in.shape[0]
    nleft = lr_in.shape[0]
    pending = []
    fetch = pltpu.make_async_copy(x_in, x, x_s)
    fetch.start()

    def put(src, dst, ssem, rsem, dev, pred=None):
        def copy():
            return pltpu.make_async_remote_copy(
                src_ref=src(), dst_ref=dst(), send_sem=ssem(), recv_sem=rsem(),
                device_id=dev, device_id_type=MESH,
            )

        run(pred, lambda: copy().start())
        pending.append((pred, lambda: copy().wait_send()))

    def got(dst, rsem, pred=None):
        def wait():
            pltpu.make_async_remote_copy(
                src_ref=dst(), dst_ref=dst(), send_sem=rsem(), recv_sem=rsem(),
                device_id={"col": c_next}, device_id_type=MESH,
            ).wait_recv()

        run(pred, wait)

    barrier = pltpu.get_barrier_semaphore()

    def greet(dev, pred=None):
        run(pred, lambda: pl.semaphore_signal(barrier, inc=1, device_id=dev, device_id_type=MESH))

    for d in range(1, R):
        greet({"row": lax.rem(r + d, R)})
    greet({"col": c_next})
    greet({"col": c_prev})
    greet({"col": c_up}, can_up)
    greet({"col": c_down}, can_down)
    pl.semaphore_wait(barrier, R + 1 + can_up.astype(jnp.int32) + can_down.astype(jnp.int32))

    peers = [lax.rem(r + 2 * d, R) for d in range(1, R // 2)]
    sib = r + 1 - 2 * lax.rem(r, 2)

    def round_rows(src, buf, ss, rs):
        for d, q in enumerate(peers):
            put(src, lambda: buf.at[r], lambda d=d: ss.at[d], lambda: rs.at[r], {"row": q})
        put(src, lambda: buf.at[r], lambda: ss.at[R // 2 - 1], lambda: rs.at[r], {"row": sib})

    def to_sibling(buf, ss, rs):
        for d, q in enumerate(peers):
            got(lambda: buf.at[q], lambda: rs.at[q])
            put(lambda q=q: buf.at[q], lambda q=q: buf.at[q], lambda d=d: ss.at[R // 2 + d],
                lambda q=q: rs.at[q], {"row": sib})

    def from_sibling(buf, rs):
        for q in [sib] + [lax.rem(sib + 2 * d, R) for d in range(1, R // 2)]:
            got(lambda: buf.at[q], lambda: rs.at[q])

    round_rows(lambda: rr_in, rr, rr_s, rr_r)

    def lr_put(src, j, k, dev, pred):
        put(src, lambda: lr.at[j], lambda: lr_s.at[k, j], lambda: lr_r.at[j], {"col": dev}, pred)

    def lo_put(src, j, k, dev, pred):
        put(src, lambda: lo.at[j], lambda: lo_s.at[k, j], lambda: lo_r.at[j], {"col": dev}, pred)

    def nl_put(src, j, pred):
        put(src, lambda: nl.at[j], lambda: nl_s.at[j], lambda: nl_r.at[j], {"row": r_prev}, pred)

    lr_put(lambda: lr_in, c, 2, mate, None)
    lr_put(lambda: lr_in, c, 0, c_up, can_up)
    lr_put(lambda: lr_in, c, 1, c_down, can_down)
    put(lambda: ro_in.at[0, :, pl.ds(0, half)], lambda: nx.at[r], lambda: nx_s.at[R - 1],
        lambda: nx_r.at[r], {"col": c_prev})
    round_rows(lambda: ro_in, ro, ro_s, ro_r)
    lo_put(lambda: lo_in, c, 2, mate, None)
    nl_put(lambda: lo_in.at[0, :, pl.ds(0, half)], c, None)
    rr[r] = rr_in[...]
    ro[r] = ro_in[...]
    lr[c] = lr_in[...]
    lo[c] = lo_in[...]

    def lr_pass(j, k, dev, pred):
        lr_put(lambda: lr.at[j], j, k, dev, pred)

    def lr_step(s, par):
        below, above = line - 1 - s, line + 1 + s
        jb = lax.rem(2 * below + par + 2 * C, C)
        ja = lax.rem(2 * above + par, C)
        has_b, has_a = below >= 0, above <= L - 1
        got(lambda: lr.at[jb], lambda: lr_r.at[jb], has_b)
        lr_pass(jb, 0, c_up, both(has_b, can_up))
        got(lambda: lr.at[ja], lambda: lr_r.at[ja], has_a)
        lr_pass(ja, 1, c_down, both(has_a, can_down))

    def lo_step(s):
        below, above = line - 1 - s, line + 1 + s
        jb = lax.rem(2 * below + y + 2 * C, C)
        ja = lax.rem(2 * above + y, C)
        has_b, has_a = below >= 0, above <= L - 1
        for j, has, k, dev, can in (
            (jb, has_b, 0, c_up, can_up), (ja, has_a, 1, c_down, can_down),
        ):
            got(lambda: lo.at[j], lambda: lo_r.at[j], has)
            lo_put(lambda j=j: lo.at[j], j, 2, mate, has)
            lo_put(lambda j=j: lo.at[j], j, k, dev, both(has, can))
            nl_put(lambda j=j: lo.at[j, 0, :, pl.ds(0, half)], j, has)

    to_sibling(rr, rr_s, rr_r)
    got(lambda: lr.at[mate], lambda: lr_r.at[mate])
    lr_pass(mate, 0, c_up, can_up)
    lr_pass(mate, 1, c_down, can_down)
    lr_step(0, y)

    from_sibling(rr, rr_r)
    for w in range(nr):
        h, l = split(rr[:, w].reshape(win, win))
        rr_h[w] = h
        rr_l[w] = l
    n_chunks = rows // chunk

    def span(i):
        return pl.ds(pl.multiple_of(i * chunk, chunk), chunk)

    def halo_copies(i):
        right = pltpu.make_async_remote_copy(
            src_ref=m.at[span(i), pl.ds(cols - half, half)], dst_ref=hp.at[span(i), :],
            send_sem=hp_s.at[i], recv_sem=hp_r.at[i],
            device_id={"col": c_next}, device_id_type=MESH)
        left = pltpu.make_async_remote_copy(
            src_ref=m.at[span(i), pl.ds(0, half)], dst_ref=hn.at[span(i), :],
            send_sem=hn_s.at[i], recv_sem=hn_r.at[i],
            device_id={"col": c_prev}, device_id_type=MESH)
        return right, left

    odd = lax.rem(r, 2)

    def turn(i, n):
        return i + odd * (n - 1 - 2 * i)

    def right_chunk(i, carry):
        i = turn(i, n_chunks)
        for w in range(nr):
            a = split(x[span(i), pl.ds(w * win, win)])
            m[span(i), pl.ds(w * win, win)] = dot3(a, (rr_h[w], rr_l[w]), RIGHT)
        for copy in halo_copies(i):
            copy.start()
        return carry

    fetch.wait()
    lax.fori_loop(0, n_chunks, right_chunk, 0)

    got(lambda: nx.at[r], lambda: nx_r.at[r])
    round_rows(lambda: nx.at[r], nx, nx_s, nx_r)

    lr_step(0, 1 - y)
    lo_put(lambda: lo_in, c, 0, c_up, can_up)
    lo_put(lambda: lo_in, c, 1, c_down, can_down)
    to_sibling(ro, ro_s, ro_r)
    lo_step(0)
    to_sibling(nx, nx_s, nx_r)
    for s in range(1, L - 2):
        lr_step(s, y)
        lr_step(s, 1 - y)

    from_sibling(ro, ro_r)
    from_sibling(nx, nx_r)
    for w in range(nr):
        h, l = split(ro[:, w].reshape(win, win))
        ro_h[w] = h
        ro_l[w] = l
    h, l = split(nx[...].reshape(win, half))
    nx_h[...] = h
    nx_l[...] = l

    def shifted_chunk(i, carry):
        i = turn(i, n_chunks)
        right, left = halo_copies(i)
        right.wait_recv()
        first = split(m[span(i), pl.ds(0, half)])
        ahead = split(hp[span(i), :])
        top = (ro_h[0, :half, half:], ro_l[0, :half, half:])
        low = (ro_h[0, half:, half:], ro_l[0, half:, half:])
        m2[span(i), pl.ds(0, half)] = dot3(ahead, top, RIGHT) + dot3(first, low, RIGHT)
        for w in range(1, nr):
            a = split(m[span(i), pl.ds(w * win - half, win)])
            m2[span(i), pl.ds(w * win - half, win)] = dot3(a, (ro_h[w], ro_l[w]), RIGHT)
        left.wait_recv()
        last = split(m[span(i), pl.ds(cols - half, half)])
        after = split(hn[span(i), :])
        top = (nx_h[:half, :], nx_l[:half, :])
        low = (nx_h[half:, :], nx_l[half:, :])
        m2[span(i), pl.ds(cols - half, half)] = dot3(last, top, RIGHT) + dot3(after, low, RIGHT)
        return carry

    per = win // chunk
    lax.fori_loop(0, per, shifted_chunk, 0)
    if L > 2:
        lr_step(L - 2, y)
        lo_step(1)
        lr_step(L - 2, 1 - y)

    def left_window(k, carry):
        k = turn(k, nleft)
        at = pl.ds(pl.multiple_of(k * win, win), win)
        q = split(lr[:, k].reshape(win, win))
        for w in range(cols // win):
            across = pl.ds(w * win, win)
            m3[at, across] = dot3(q, split(m2[at, across]), LEFT)
        return carry

    def rows_up(pred):
        put(lambda: m3.at[pl.ds(rows - half, half), :], lambda: ha, lambda: hr_s.at[0],
            lambda: hr_r.at[0], {"row": r_next}, pred)

    def rows_down(pred):
        put(lambda: m3.at[pl.ds(0, half), :], lambda: hb, lambda: hr_s.at[1],
            lambda: hr_r.at[1], {"row": r_prev}, pred)

    left_window(0, 0)
    rows_down(odd == 0)
    rows_up(odd == 1)
    def other_windows():
        for k in range(1, nleft):
            lax.fori_loop(k * per, (k + 1) * per, shifted_chunk, 0)
            left_window(k, 0)
        rows_up(odd == 0)
        rows_down(odd == 1)

    other_windows()
    for s in range(2, L - 1):
        lo_step(s)

    strip = win // C

    def stack(ref, at, par):
        return jnp.concatenate(
            [ref[pl.ds(pl.multiple_of(at + (2 * g + par) * strip, strip), strip), :]
             for g in range(L // 2)], axis=0)

    def product(q, parts, at, add):
        b = split(jnp.concatenate(parts, axis=0))
        res = dot3(split(q), b, LEFT)
        out[at, :] = out[at, :] + res if add else res

    def off(k, par, lo_cut, hi_cut):
        return jnp.concatenate([lo[2 * g + par, k, :, lo_cut:hi_cut] for g in range(L)], axis=0)

    def middle(par, add):
        for k in range(1, nleft):
            base = k * win - half
            product(off(k, par, 0, win),
                    [stack(m3, base, par), stack(m3, k * win, par)], pl.ds(base, win), add)

    def leading(par, add):
        product(off(0, par, half, win),
                [stack(ha, 0, par), stack(m3, 0, par)], pl.ds(0, half), add)

    def trailing(par, add):
        q = jnp.concatenate([nl[2 * g + par] for g in range(L)], axis=0)
        product(q, [stack(m3, rows - half, par), stack(hb, 0, par)],
                pl.ds(rows - half, half), add)

    middle(y, False)
    got(lambda: ha, lambda: hr_r.at[0])
    leading(y, False)
    for g in range(L):
        j = 2 * g + y
        got(lambda: nl.at[j], lambda: nl_r.at[j])
    got(lambda: hb, lambda: hr_r.at[1])
    trailing(y, False)
    for g in range(L):
        j = 2 * g + 1 - y
        got(lambda: lo.at[j], lambda: lo_r.at[j])
        nl_put(lambda j=j: lo.at[j, 0, :, pl.ds(0, half)], j, None)
    middle(1 - y, True)
    leading(1 - y, True)
    for g in range(L):
        j = 2 * g + 1 - y
        got(lambda: nl.at[j], lambda: nl_r.at[j])
    trailing(1 - y, True)

    def sent(i, carry):
        for copy in halo_copies(i):
            copy.wait_send()
        return carry

    lax.fori_loop(0, n_chunks, sent, 0)
    for pred, wait in pending:
        run(pred, wait)


def solution(mesh):
    R, C = mesh.shape["row"], mesh.shape["col"]

    def body(schur, left_rot, right_rot, left_off, right_off):
        rows, cols = schur.shape
        win = left_rot.shape[2]
        half = win // 2
        nr, nleft = right_rot.shape[0], left_rot.shape[0]
        chunk = half
        n_chunks = rows // chunk
        dma = pltpu.SemaphoreType.DMA
        vm = pltpu.VMEM
        right = (R,) + right_rot.shape
        left = (C,) + left_rot.shape
        return pl.pallas_call(
            functools.partial(kernel, R, C, chunk),
            out_shape=jax.ShapeDtypeStruct((rows, cols), F32),
            in_specs=[pl.BlockSpec(memory_space=pl.ANY)] + [pl.BlockSpec(memory_space=vm)] * 4,
            out_specs=pl.BlockSpec(memory_space=vm),
            scratch_shapes=[
                vm((rows, cols), F32), vm(right, F32), vm(right, F32), vm((R, win // R, half), F32),
                vm(left, F32), vm(left, F32), vm((C, win // C, half), F32),
                vm((rows, cols), F32), vm((rows, cols), F32), vm((rows, cols), F32),
                vm((rows, half), F32), vm((rows, half), F32),
                vm((half, cols), F32), vm((half, cols), F32),
                vm((nr, win, win), BF16), vm((nr, win, win), BF16),
                vm((nr, win, win), BF16), vm((nr, win, win), BF16),
                vm((win, half), BF16), vm((win, half), BF16),
                dma((R,)), dma((R,)), dma((R,)), dma((R,)), dma((R,)), dma((R,)),
                dma((3, C)), dma((C,)), dma((3, C)), dma((C,)), dma((C,)), dma((C,)),
                dma((n_chunks,)), dma((n_chunks,)), dma((n_chunks,)), dma((n_chunks,)),
                dma((2,)), dma((2,)), dma,
            ],
            compiler_params=pltpu.CompilerParams(collective_id=0, has_side_effects=True),
        )(schur, right_rot, right_off, left_rot, left_off)

    return jax.shard_map(
        body,
        mesh=mesh,
        in_specs=(
            P("row", "col"),
            P("row", "col", None),
            P("col", "row", None),
            P("row", "col", None),
            P("col", "row", None),
        ),
        out_specs=P("row", "col"),
        check_vma=False,
    )
```

profile of v0, /device:TPU:1, one launch (start us, length us, event | category | flops | bytes accessed | tf_op | source)
XLA Modules:
  0.0 99.4 jit_solution(310318857101131932)
XLA Ops:
  0.0 96.3 %shard_map.55 = f32[1024,512]{1,0:T(8,128)} custom-call(f32[1024,512]{1,0:T(8,128)} %x_in.1, f32[1,128,512]{2,1,0:T(8,128)} %rr_in.1, f32[1,128,512]{2,1,0:T(8,128)} %ro_in.1, f32[2,64,512]{2,1,0:T(8,128)} %lr_in.1, f32[2,64,512]{2,1,0:T(8,128)} %lo_in.1), custom_call_target="tpu_custom_call" | custom-call | tf_op jit(solution)/shard_map/pallas_call | solution.py:371
  96.3 3.1 %copy.7 = f32[1024,512]{1,0:T(8,128)} copy(f32[1024,512]{1,0:T(8,128)} %shard_map.55) | data formatting | bytes 4194304
where the time goes:
time: 99.5 us; the launch traced here: 99.4 us
  Pallas kernels  96.3 us (97%)
  local copies, waits for them, and re-layouts  3.08 us (3%)
    pallas_call x1, Pallas kernels, body(): pl.pallas_call(functools.partial(kernel, R, C, chunk), out_shape=jax.Shap...  96.3 us
    unnamed x1, local copies, waits for them, and re-layouts  3.08 us

commit v1 on v0

v1 whole, which is shorter than its diff:
```python
import functools

import jax
import jax.numpy as jnp
from jax import lax
from jax.experimental import pallas as pl
from jax.experimental.pallas import tpu as pltpu
from jax.sharding import PartitionSpec as P

MESH = pl.DeviceIdType.MESH
F32 = jnp.float32
BF16 = jnp.bfloat16


def run(pred, fn):
    if pred is None:
        fn()
    else:
        pl.when(pred)(fn)


def both(a, b):
    if a is None:
        return b
    if b is None:
        return a
    return jnp.logical_and(a, b)


def split(v):
    high = v.astype(BF16)
    return high, (v - high.astype(F32)).astype(BF16)


def dot3(a, b, dims):
    def one(p, q):
        return lax.dot_general(p, q, (dims, ((), ())), preferred_element_type=F32)

    return one(a[0], b[0]) + (one(a[0], b[1]) + one(a[1], b[0]))


DETOUR = 0
SHORT = 1
RIGHT = ((1,), (0,))
LEFT = ((0,), (0,))


def kernel(
    R, C, chunk, detour,
    x_in, rr_in, ro_in, lr_in, lo_in, out,
    x, rr, ro, nx, lr, lo, nl, m, m2, m3, hp, hn, hx, ha, hb,
    rr_h, rr_l, ro_h, ro_l, nx_h, nx_l,
    rr_s, rr_r, ro_s, ro_r, nx_s, nx_r, lr_s, lr_r, lo_s, lo_r, nl_s, nl_r,
    hp_s, hp_r, hn_s, hn_r, hx_s, hx_r, hr_s, hr_r, x_s,
):
    r = lax.axis_index("row")
    c = lax.axis_index("col")
    L = C // 2
    line = lax.div(c, 2)
    y = lax.rem(c, 2)
    mate = 2 * line + 1 - y
    c_next, c_prev = lax.rem(c + 1, C), lax.rem(c + C - 1, C)
    r_next, r_prev = lax.rem(r + 1, R), lax.rem(r + R - 1, R)
    can_up, can_down = line < L - 1, line > 0
    in_up, in_down = line < L - 2, line > 1
    at_end = jnp.logical_or(line == 0, line == L - 1)
    c_up, c_down = lax.rem(c + 2, C), lax.rem(c + C - 2, C)
    rows, cols = x.shape
    win = lr_in.shape[2]
    half = win // 2
    nr = rr_in.shape[0]
    nleft = lr_in.shape[0]
    pending = []
    fetch = pltpu.make_async_copy(x_in, x, x_s)
    fetch.start()

    around = functools.reduce(jnp.logical_or, [c == 0, c == 2, c == C - 3, c == C - 1])
    via = jnp.where(c == 0, C - 3, jnp.where(c == 2, 3, jnp.where(c == C - 3, C - 4, 2)))
    low_relay = jnp.logical_or(c == 2, c == 3)
    relays = jnp.logical_or(low_relay, jnp.logical_or(c == C - 4, c == C - 3))
    onward = jnp.where(low_relay, c_down, c_up)

    def put(src, dst, ssem, rsem, dev, pred=None):
        def copy():
            return pltpu.make_async_remote_copy(
                src_ref=src(), dst_ref=dst(), send_sem=ssem(), recv_sem=rsem(),
                device_id=dev, device_id_type=MESH,
            )

        run(pred, lambda: copy().start())
        pending.append((pred, lambda: copy().wait_send()))

    def got(dst, rsem, pred=None):
        def wait():
            pltpu.make_async_remote_copy(
                src_ref=dst(), dst_ref=dst(), send_sem=rsem(), recv_sem=rsem(),
                device_id={"col": c_next}, device_id_type=MESH,
            ).wait_recv()

        run(pred, wait)

    barrier = pltpu.get_barrier_semaphore()

    def greet(dev, pred=None):
        run(pred, lambda: pl.semaphore_signal(barrier, inc=1, device_id=dev, device_id_type=MESH))

    for d in range(1, R):
        greet({"row": lax.rem(r + d, R)})
    greet({"col": c_next})
    greet({"col": c_prev})
    greet({"col": c_up}, can_up)
    greet({"col": c_down}, can_down)
    callers = R + 1 + can_up.astype(jnp.int32) + can_down.astype(jnp.int32)
    if detour:
        for one, other in ((0, C - 3), (C - 1, 2)):
            greet({"col": other}, c == one)
            greet({"col": one}, c == other)
            callers = callers + jnp.logical_or(c == one, c == other).astype(jnp.int32)
    pl.semaphore_wait(barrier, callers)

    peers = [lax.rem(r + 2 * d, R) for d in range(1, R // 2)]
    sib = r + 1 - 2 * lax.rem(r, 2)

    def round_rows(src, buf, ss, rs):
        for d, q in enumerate(peers):
            put(src, lambda: buf.at[r], lambda d=d: ss.at[d], lambda: rs.at[r], {"row": q})
        put(src, lambda: buf.at[r], lambda: ss.at[R // 2 - 1], lambda: rs.at[r], {"row": sib})

    def to_sibling(buf, ss, rs):
        for d, q in enumerate(peers):
            got(lambda: buf.at[q], lambda: rs.at[q])
            put(lambda q=q: buf.at[q], lambda q=q: buf.at[q], lambda d=d: ss.at[R // 2 + d],
                lambda q=q: rs.at[q], {"row": sib})

    def from_sibling(buf, rs):
        for q in [sib] + [lax.rem(sib + 2 * d, R) for d in range(1, R // 2)]:
            got(lambda: buf.at[q], lambda: rs.at[q])

    class Gather:
        def __init__(self, own, buf, ss, rs):
            self.own, self.buf, self.ss, self.rs = own, buf, ss, rs
            self.waited = []

        def send(self, j, w, k, pred, own=False):
            src = (lambda: self.own.at[w]) if own else (lambda: self.buf.at[j, w])
            put(src, lambda: self.buf.at[j, w], lambda: self.ss.at[k, j, w],
                lambda: self.rs.at[j, w], {"col": (c_up, c_down, mate)[k]}, pred)

        def wait(self, j, w, pred=None):
            got(lambda: self.buf.at[j, w], lambda: self.rs.at[j, w], pred)

    lr_g = Gather(lr_in, lr, lr_s, lr_r)
    lo_g = Gather(lo_in, lo, lo_s, lo_r)

    def source(side, d, own):
        plane = line - d if side == 0 else line + d
        has = plane >= 0 if side == 0 else plane <= L - 1
        return lax.rem(2 * plane + (y if own else 1 - y) + 2 * C, C), has

    def onwards(g, side, d, own, w):
        can, inner = ((can_up, in_up), (can_down, in_down))[side]
        j, has = source(side, d, own)
        along = both(has, can if own or g is lr_g else inner)
        across = None
        if own and (g is lo_g or (d == 1 and w < SHORT)):
            across = both(has, at_end)
        return j, has, along, across

    def nl_put(j, pred, own=False):
        src = lo_in.at[0, :, pl.ds(0, half)] if own else None
        put(lambda: src if own else lo.at[j, 0, :, pl.ds(0, half)], lambda: nl.at[j],
            lambda: nl_s.at[j], lambda: nl_r.at[j], {"row": r_prev}, pred)

    def relay(g, d, own, w):
        for side in (0, 1):
            if d == L - 1:
                use = jnp.bool_(False)
            j, has, along, across = onwards(g, side, d, own, w)
            use = along if across is None else jnp.logical_or(along, across)
            if d == L - 1 and across is None:
                continue
            g.wait(j, w, use)
            g.send(j, w, side, along)
            if across is not None:
                g.send(j, w, 2, across)
            if g is lo_g and w == 0:
                nl_put(j, use)

    def settle(g, w):
        for d in range(1, L):
            for own in (True, False):
                for side in (0, 1):
                    j, has, along, across = onwards(g, side, d, own, w)
                    use = along if across is None else jnp.logical_or(along, across)
                    rest = has if d == L - 1 and across is None else both(has, jnp.logical_not(use))
                    g.wait(j, w, rest)
                    if g is lo_g and w == 0:
                        nl_put(j, rest)

    round_rows(lambda: rr_in, rr, rr_s, rr_r)
    for w in range(nleft):
        lr_g.send(c, w, 2, None, True)
        lr_g.send(c, w, 0, can_up, True)
        lr_g.send(c, w, 1, can_down, True)
    put(lambda: ro_in.at[0, :, pl.ds(0, half)], lambda: nx.at[r], lambda: nx_s.at[R - 1],
        lambda: nx_r.at[r], {"col": c_prev})
    round_rows(lambda: ro_in, ro, ro_s, ro_r)
    for w in range(nleft):
        lo_g.send(c, w, 2, None, True)
    nl_put(c, None, True)
    rr[r] = rr_in[...]
    ro[r] = ro_in[...]
    lr[c] = lr_in[...]
    lo[c] = lo_in[...]

    for w in range(nleft):
        lr_g.wait(mate, w)
        lr_g.send(mate, w, 0, in_up if w < SHORT else can_up)
        lr_g.send(mate, w, 1, in_down if w < SHORT else can_down)
        relay(lr_g, 1, True, w)
    to_sibling(rr, rr_s, rr_r)
    from_sibling(rr, rr_r)
    for w in range(nr):
        h, l = split(rr[:, w].reshape(win, win))
        rr_h[w] = h
        rr_l[w] = l
    n_chunks = rows // chunk
    odd = lax.rem(r, 2)

    def turn(i, n):
        return i + odd * (n - 1 - 2 * i)

    def span(i):
        return pl.ds(pl.multiple_of(i * chunk, chunk), chunk)

    def halo(i, forward, n=None):
        cut = pl.ds(cols - half, half) if forward else pl.ds(0, half)
        dst, ss, rs = (hp, hp_s, hp_r) if forward else (hn, hn_s, hn_r)
        if n is None:
            return pltpu.make_async_remote_copy(
                src_ref=m.at[span(i), cut], dst_ref=dst.at[span(i), :],
                send_sem=ss.at[i], recv_sem=rs.at[i],
                device_id={"col": c_next if forward else c_prev}, device_id_type=MESH)
        return pltpu.make_async_remote_copy(
            src_ref=m.at[span(i), cut], dst_ref=hx.at[n],
            send_sem=ss.at[i], recv_sem=hx_r.at[n],
            device_id={"col": via}, device_id_type=MESH)

    def far_start(i, n):
        for forward in (True, False):
            far = y == (1 if forward else 0)
            if n is None:
                run(far, lambda: halo(i, forward).start())
            else:
                run(both(far, around), lambda: halo(i, forward, n).start())
                run(both(far, jnp.logical_not(around)), lambda: halo(i, forward).start())

    def near_start(i):
        for forward in (True, False):
            run(y == (0 if forward else 1), lambda: halo(i, forward).start())

    def right_chunk(i):
        for w in range(nr):
            a = split(x[span(i), pl.ds(w * win, win)])
            m[span(i), pl.ds(w * win, win)] = dot3(a, (rr_h[w], rr_l[w]), RIGHT)

    fetch.wait()
    for n in range(n_chunks):
        i = turn(n, n_chunks)
        right_chunk(i)
        far_start(i, n if n < detour else None)
        if n >= detour:
            near_start(i)
        if n == detour - 1:
            for k in range(detour):
                near_start(turn(k, n_chunks))

    def hx_copy(n):
        i = turn(n, n_chunks)
        even = pltpu.make_async_remote_copy(
            src_ref=hx.at[n], dst_ref=hp.at[span(i), :], send_sem=hx_s.at[n], recv_sem=hp_r.at[i],
            device_id={"col": onward}, device_id_type=MESH)
        uneven = pltpu.make_async_remote_copy(
            src_ref=hx.at[n], dst_ref=hn.at[span(i), :], send_sem=hx_s.at[n], recv_sem=hn_r.at[i],
            device_id={"col": onward}, device_id_type=MESH)
        return even, uneven

    def hx_relay(n):
        got(lambda: hx.at[n], lambda: hx_r.at[n], relays)
        even, uneven = hx_copy(n)
        run(both(relays, y == 0), even.start)
        run(both(relays, y == 1), uneven.start)

    got(lambda: nx.at[r], lambda: nx_r.at[r])
    round_rows(lambda: nx.at[r], nx, nx_s, nx_r)
    for w in range(nleft):
        relay(lr_g, 1, False, w)
    for w in range(nleft):
        lo_g.send(c, w, 0, can_up, True)
        lo_g.send(c, w, 1, can_down, True)
    to_sibling(ro, ro_s, ro_r)
    to_sibling(nx, nx_s, nx_r)
    for n in range(detour):
        hx_relay(n)
    for d in range(2, L):
        for own in (True, False):
            for w in range(nleft):
                relay(lr_g, d, own, w)

    def lo_mate(w):
        lo_g.wait(mate, w)
        lo_g.send(mate, w, 0, in_up)
        lo_g.send(mate, w, 1, in_down)
        if w == 0:
            nl_put(mate, None)

    from_sibling(ro, ro_r)
    from_sibling(nx, nx_r)
    for w in range(nr):
        h, l = split(ro[:, w].reshape(win, win))
        ro_h[w] = h
        ro_l[w] = l
    h, l = split(nx[...].reshape(win, half))
    nx_h[...] = h
    nx_l[...] = l
    for w in range(nleft):
        lo_mate(w)

    def shifted_chunk(i):
        got(lambda: hp.at[span(i), :], lambda: hp_r.at[i])
        first = split(m[span(i), pl.ds(0, half)])
        ahead = split(hp[span(i), :])
        top = (ro_h[0, :half, half:], ro_l[0, :half, half:])
        low = (ro_h[0, half:, half:], ro_l[0, half:, half:])
        m2[span(i), pl.ds(0, half)] = dot3(ahead, top, RIGHT) + dot3(first, low, RIGHT)
        for w in range(1, nr):
            a = split(m[span(i), pl.ds(w * win - half, win)])
            m2[span(i), pl.ds(w * win - half, win)] = dot3(a, (ro_h[w], ro_l[w]), RIGHT)
        got(lambda: hn.at[span(i), :], lambda: hn_r.at[i])
        last = split(m[span(i), pl.ds(cols - half, half)])
        after = split(hn[span(i), :])
        top = (nx_h[:half, :], nx_l[:half, :])
        low = (nx_h[half:, :], nx_l[half:, :])
        m2[span(i), pl.ds(cols - half, half)] = dot3(last, top, RIGHT) + dot3(after, low, RIGHT)

    per = win // chunk

    def left_window(k):
        k = turn(k, nleft)
        at = pl.ds(pl.multiple_of(k * win, win), win)
        q = split(lr[:, k].reshape(win, win))
        for w in range(cols // win):
            across = pl.ds(w * win, win)
            m3[at, across] = dot3(q, split(m2[at, across]), LEFT)

    def rows_up(pred):
        put(lambda: m3.at[pl.ds(rows - half, half), :], lambda: ha, lambda: hr_s.at[0],
            lambda: hr_r.at[0], {"row": r_next}, pred)

    def rows_down(pred):
        put(lambda: m3.at[pl.ds(0, half), :], lambda: hb, lambda: hr_s.at[1],
            lambda: hr_r.at[1], {"row": r_prev}, pred)

    for n in range(per):
        shifted_chunk(turn(n, n_chunks))
    for own in (True, False):
        relay(lo_g, 1, own, 0)
    for w in range(nleft):
        settle(lr_g, w)
    left_window(0)
    rows_down(odd == 0)
    rows_up(odd == 1)
    for w in range(1, nleft):
        for own in (True, False):
            relay(lo_g, 1, own, w)
    for k in range(1, nleft):
        for n in range(k * per, (k + 1) * per):
            shifted_chunk(turn(n, n_chunks))
        left_window(k)
    rows_up(odd == 0)
    rows_down(odd == 1)
    for w in range(nleft):
        for d in range(2, L):
            for own in (True, False):
                relay(lo_g, d, own, w)

    strip = win // C

    def store(q, parts, at, add):
        res = dot3(split(q), split(jnp.concatenate(parts, axis=0)), LEFT)
        out[at, :] = out[at, :] + res if add else res

    settle(lo_g, 0)
    got(lambda: ha, lambda: hr_r.at[0])
    store(lo[:, 0, :, half:].reshape(win, half), [ha[...], m3[pl.ds(0, half), :]],
          pl.ds(0, half), False)
    for j in range(C):
        got(lambda: nl.at[j], lambda: nl_r.at[j])
    got(lambda: hb, lambda: hr_r.at[1])
    store(nl[...].reshape(win, half), [m3[pl.ds(rows - half, half), :], hb[...]],
          pl.ds(rows - half, half), False)
    for w in range(1, nleft):
        settle(lo_g, w)
        base = w * win - half
        store(lo[:, w].reshape(win, win), [m3[pl.ds(base, win), :]], pl.ds(base, win), False)

    for n in range(n_chunks):
        i = turn(n, n_chunks)
        for forward in (True, False):
            halo(i, forward).wait_send()
        if n < detour:
            run(relays, hx_copy(n)[0].wait_send)
    for pred, wait in pending:
        run(pred, wait)


def solution(mesh):
    R, C = mesh.shape["row"], mesh.shape["col"]

    def body(schur, left_rot, right_rot, left_off, right_off):
        rows, cols = schur.shape
        win = left_rot.shape[2]
        half = win // 2
        nr, nleft = right_rot.shape[0], left_rot.shape[0]
        chunk = half
        n_chunks = rows // chunk
        dma = pltpu.SemaphoreType.DMA
        vm = pltpu.VMEM
        right = (R,) + right_rot.shape
        left = (C,) + left_rot.shape
        return pl.pallas_call(
            functools.partial(kernel, R, C, chunk, DETOUR),
            out_shape=jax.ShapeDtypeStruct((rows, cols), F32),
            in_specs=[pl.BlockSpec(memory_space=pl.ANY)] + [pl.BlockSpec(memory_space=vm)] * 4,
            out_specs=pl.BlockSpec(memory_space=vm),
            scratch_shapes=[
                vm((rows, cols), F32), vm(right, F32), vm(right, F32), vm((R, win // R, half), F32),
                vm(left, F32), vm(left, F32), vm((C, win // C, half), F32),
                vm((rows, cols), F32), vm((rows, cols), F32), vm((rows, cols), F32),
                vm((rows, half), F32), vm((rows, half), F32),
                vm((max(DETOUR, 1), chunk, half), F32),
                vm((half, cols), F32), vm((half, cols), F32),
                vm((nr, win, win), BF16), vm((nr, win, win), BF16),
                vm((nr, win, win), BF16), vm((nr, win, win), BF16),
                vm((win, half), BF16), vm((win, half), BF16),
                dma((R,)), dma((R,)), dma((R,)), dma((R,)), dma((R,)), dma((R,)),
                dma((3, C, nleft)), dma((C, nleft)), dma((3, C, nleft)), dma((C, nleft)), dma((C,)), dma((C,)),
                dma((n_chunks,)), dma((n_chunks,)), dma((n_chunks,)), dma((n_chunks,)),
                dma((max(DETOUR, 1),)), dma((max(DETOUR, 1),)),
                dma((2,)), dma((2,)), dma,
            ],
            compiler_params=pltpu.CompilerParams(collective_id=0, has_side_effects=True),
        )(schur, right_rot, right_off, left_rot, left_off)

    return jax.shard_map(
        body,
        mesh=mesh,
        in_specs=(
            P("row", "col"),
            P("row", "col", None),
            P("col", "row", None),
            P("row", "col", None),
            P("col", "row", None),
        ),
        out_specs=P("row", "col"),
        check_vma=False,
    )
```

time: 99.5 us -> 93.3 us (0.938)
  Pallas kernels: 96.3 us -> 90 us
    pallas_call x1, Pallas kernels: 96.3 us -> 90 us  [body(): pl.pallas_call(functools.partial(kernel, R, C, chunk, DETOUR), out_shape=...]
where the time goes in v1:
time: 93.3 us; the launch traced here: 93.1 us
  Pallas kernels  90 us (96%)
  local copies, waits for them, and re-layouts  3.08 us (3%)
    pallas_call x1, Pallas kernels, body(): pl.pallas_call(functools.partial(kernel, R, C, chunk, DETOUR), out_shape=...  90 us
    unnamed x1, local copies, waits for them, and re-layouts  3.08 us

profile of v1, /device:TPU:1, one launch (start us, length us, event | category | flops | bytes accessed | tf_op | source)
XLA Modules:
  0.0 93.1 jit_solution(1086678383590997508)
XLA Ops:
  0.0 90.0 %shard_map.55 = f32[1024,512]{1,0:T(8,128)} custom-call(f32[1024,512]{1,0:T(8,128)} %x_in.1, f32[1,128,512]{2,1,0:T(8,128)} %rr_in.1, f32[1,128,512]{2,1,0:T(8,128)} %ro_in.1, f32[2,64,512]{2,1,0:T(8,128)} %lr_in.1, f32[2,64,512]{2,1,0:T(8,128)} %lo_in.1), custom_call_target="tpu_custom_call" | custom-call | tf_op jit(solution)/shard_map/pallas_call | solution.py:431
  90.0 3.1 %copy.7 = f32[1024,512]{1,0:T(8,128)} copy(f32[1024,512]{1,0:T(8,128)} %shard_map.55) | data formatting | bytes 4194304

commit v2 on v1

--- a/solution.py
+++ b/solution.py
@@ -51,7 +51,7 @@
     x, rr, ro, nx, lr, lo, nl, m, m2, m3, hp, hn, hx, ha, hb,
     rr_h, rr_l, ro_h, ro_l, nx_h, nx_l,
     rr_s, rr_r, ro_s, ro_r, nx_s, nx_r, lr_s, lr_r, lo_s, lo_r, nl_s, nl_r,
-    hp_s, hp_r, hn_s, hn_r, hx_s, hx_r, hr_s, hr_r, x_s,
+    hp_s, hp_r, hn_s, hn_r, hx_s, hx_r, hr_s, hr_r, x_s, o_s, tok,
 ):
     r = lax.axis_index("row")
     c = lax.axis_index("col")
@@ -72,7 +72,10 @@
     nleft = lr_in.shape[0]
     pending = []
     fetch = pltpu.make_async_copy(x_in, x, x_s)
-    fetch.start()
+    owns = [pltpu.make_async_copy(a, b, o_s.at[n]) for n, (a, b) in enumerate(
+        ((rr_in, rr.at[r]), (ro_in, ro.at[r]), (lr_in, lr.at[c]), (lo_in, lo.at[c])))]
+    for copy in [owns[0], fetch] + owns[1:]:
+        copy.start()
 
     around = functools.reduce(jnp.logical_or, [c == 0, c == 2, c == C - 3, c == C - 1])
     via = jnp.where(c == 0, C - 3, jnp.where(c == 2, 3, jnp.where(c == C - 3, C - 4, 2)))
@@ -104,19 +107,26 @@
     def greet(dev, pred=None):
         run(pred, lambda: pl.semaphore_signal(barrier, inc=1, device_id=dev, device_id_type=MESH))
 
+    first, final = c == 0, c == C - 1
     for d in range(1, R):
         greet({"row": lax.rem(r + d, R)})
-    greet({"col": c_next})
-    greet({"col": c_prev})
+    greet({"col": c_next}, jnp.logical_not(final))
+    greet({"col": c_prev}, jnp.logical_not(first))
     greet({"col": c_up}, can_up)
     greet({"col": c_down}, can_down)
-    callers = R + 1 + can_up.astype(jnp.int32) + can_down.astype(jnp.int32)
-    if detour:
-        for one, other in ((0, C - 3), (C - 1, 2)):
-            greet({"col": other}, c == one)
-            greet({"col": one}, c == other)
-            callers = callers + jnp.logical_or(c == one, c == other).astype(jnp.int32)
-    pl.semaphore_wait(barrier, callers)
+    callers = R + 1 + jnp.where(can_up, 1, 0) + jnp.where(can_down, 1, 0)
+    pl.semaphore_wait(barrier, callers - jnp.where(jnp.logical_or(first, final), 1, 0))
+
+    def word(n, along, heard, c_to):
+        run(both(along, heard), lambda: pl.semaphore_wait(tok.at[n], 1))
+        run(along, lambda: pl.semaphore_signal(
+            tok.at[n], inc=1, device_id={"col": c_to}, device_id_type=MESH))
+
+    def far_ends():
+        word(0, both(y == 0, line >= 1), line >= 2, jnp.where(can_up, c_up, mate))
+        word(1, both(y == 1, line <= L - 2), line <= L - 3, jnp.where(can_down, c_down, mate))
+        run(final, lambda: pl.semaphore_wait(tok.at[0], 1))
+        run(first, lambda: pl.semaphore_wait(tok.at[1], 1))
 
     peers = [lax.rem(r + 2 * d, R) for d in range(1, R // 2)]
     sib = r + 1 - 2 * lax.rem(r, 2)
@@ -202,16 +212,15 @@
         lr_g.send(c, w, 2, None, True)
         lr_g.send(c, w, 0, can_up, True)
         lr_g.send(c, w, 1, can_down, True)
+    far_ends()
     put(lambda: ro_in.at[0, :, pl.ds(0, half)], lambda: nx.at[r], lambda: nx_s.at[R - 1],
         lambda: nx_r.at[r], {"col": c_prev})
     round_rows(lambda: ro_in, ro, ro_s, ro_r)
     for w in range(nleft):
         lo_g.send(c, w, 2, None, True)
     nl_put(c, None, True)
-    rr[r] = rr_in[...]
-    ro[r] = ro_in[...]
-    lr[c] = lr_in[...]
-    lo[c] = lo_in[...]
+    for copy in owns:
+        copy.wait()
 
     for w in range(nleft):
         lr_g.wait(mate, w)
@@ -431,7 +440,7 @@
         return pl.pallas_call(
             functools.partial(kernel, R, C, chunk, DETOUR),
             out_shape=jax.ShapeDtypeStruct((rows, cols), F32),
-            in_specs=[pl.BlockSpec(memory_space=pl.ANY)] + [pl.BlockSpec(memory_space=vm)] * 4,
+            in_specs=[pl.BlockSpec(memory_space=pltpu.HBM)] * 5,
             out_specs=pl.BlockSpec(memory_space=vm),
             scratch_shapes=[
                 vm((rows, cols), F32), vm(right, F32), vm(right, F32), vm((R, win // R, half), F32),
@@ -447,7 +456,7 @@
                 dma((3, C, nleft)), dma((C, nleft)), dma((3, C, nleft)), dma((C, nleft)), dma((C,)), dma((C,)),
                 dma((n_chunks,)), dma((n_chunks,)), dma((n_chunks,)), dma((n_chunks,)),
                 dma((max(DETOUR, 1),)), dma((max(DETOUR, 1),)),
-                dma((2,)), dma((2,)), dma,
+                dma((2,)), dma((2,)), dma, dma((4,)), pltpu.SemaphoreType.REGULAR((2,)),
             ],
             compiler_params=pltpu.CompilerParams(collective_id=0, has_side_effects=True),
         )(schur, right_rot, right_off, left_rot, left_off)

time: 93.3 us -> 92.4 us (level)
  Pallas kernels: 90 us -> 88.9 us
    pallas_call x1, Pallas kernels: 90 us -> 88.9 us  [body(): pl.pallas_call(functools.partial(kernel, R, C, chunk, DETOUR), out_shape=...]
where the time goes in v2:
time: 92.4 us; the launch traced here: 92 us
  Pallas kernels  88.9 us (96%)
  local copies, waits for them, and re-layouts  3.08 us (3%)
    pallas_call x1, Pallas kernels, body(): pl.pallas_call(functools.partial(kernel, R, C, chunk, DETOUR), out_shape=...  88.9 us
    unnamed x1, local copies, waits for them, and re-layouts  3.08 us

profile of v2, /device:TPU:1, one launch (start us, length us, event | category | flops | bytes accessed | tf_op | source)
XLA Modules:
  0.0 92.0 jit_solution(2935295054307268005)
XLA Ops:
  0.0 88.9 %shard_map.55 = f32[1024,512]{1,0:T(8,128)} custom-call(f32[1024,512]{1,0:T(8,128)} %x_in.1, f32[1,128,512]{2,1,0:T(8,128)} %rr_in.1, f32[1,128,512]{2,1,0:T(8,128)} %ro_in.1, f32[2,64,512]{2,1,0:T(8,128)} %lr_in.1, f32[2,64,512]{2,1,0:T(8,128)} %lo_in.1), custom_call_target="tpu_custom_call" | custom-call | tf_op jit(solution)/shard_map/pallas_call | solution.py:440
  88.9 3.1 %copy.7 = f32[1024,512]{1,0:T(8,128)} copy(f32[1024,512]{1,0:T(8,128)} %shard_map.55) | data formatting | bytes 4194304

commit v3 on v2

--- a/solution.py
+++ b/solution.py
@@ -458,8 +458,8 @@
                 dma((max(DETOUR, 1),)), dma((max(DETOUR, 1),)),
                 dma((2,)), dma((2,)), dma, dma((4,)), pltpu.SemaphoreType.REGULAR((2,)),
             ],
-            compiler_params=pltpu.CompilerParams(collective_id=0, has_side_effects=True),
-        )(schur, right_rot, right_off, left_rot, left_off)
+            compiler_params=pltpu.CompilerParams(collective_id=0, has_side_effects=True, vmem_limit_bytes=44 * 2**20),
+        )(*(pltpu.with_memory_space_constraint(a, pltpu.HBM) for a in (schur, right_rot, right_off, left_rot, left_off)))
 
     return jax.shard_map(
         body,

time: 92.4 us -> 89.2 us (0.965)
  local copies, waits for them, and re-layouts: 3.08 us -> 1.32 us
  Pallas kernels: 88.9 us -> 87.6 us
    unnamed x1, local copies, waits for them, and re-layouts: 3.08 us -> 1.32 us
    pallas_call x1, Pallas kernels: 88.9 us -> 87.6 us  [body(): pl.pallas_call(functools.partial(kernel, R, C, chunk, DETOUR), out_shape=...]
where the time goes in v3:
time: 89.2 us; the launch traced here: 88.9 us
  Pallas kernels  87.6 us (98%)
  local copies, waits for them, and re-layouts  1.32 us (1%)
    pallas_call x1, Pallas kernels, body(): pl.pallas_call(functools.partial(kernel, R, C, chunk, DETOUR), out_shape=...  87.6 us

profile of v3, /device:TPU:1, one launch (start us, length us, event | category | flops | bytes accessed | tf_op | source)
XLA Modules:
  0.0 88.9 jit_solution(8512663323705479233)
XLA Ops:
  0.0 87.6 %shard_map.55 = f32[1024,512]{1,0:T(8,128)S(1)} custom-call(f32[1024,512]{1,0:T(8,128)} %x_in.1, f32[1,128,512]{2,1,0:T(8,128)} %rr_in.1, f32[1,128,512]{2,1,0:T(8,128)} %ro_in.1, f32[2,64,512]{2,1,0:T(8,128)} %lr_in.1, f32[2,64,512]{2,1,0:T(8,128)} %lo_in.1), custom_call_target="tpu_custom_call" | custom-call | tf_op jit(solution)/shard_map/pallas_call | solution.py:440
  87.6 1.3 %copy.7 = f32[1024,512]{1,0:T(8,128)} copy(f32[1024,512]{1,0:T(8,128)S(1)} %shard_map.55) | data formatting | bytes 4194304

commit v4 on v3

--- a/solution.py
+++ b/solution.py
@@ -41,6 +41,7 @@
 
 DETOUR = 0
 SHORT = 1
+DIRECT = 1
 RIGHT = ((1,), (0,))
 LEFT = ((0,), (0,))
 
@@ -170,9 +171,14 @@
     def onwards(g, side, d, own, w):
         can, inner = ((can_up, in_up), (can_down, in_down))[side]
         j, has = source(side, d, own)
-        along = both(has, can if own or g is lr_g else inner)
+        reach = can if own or g is lr_g else inner
+        direct = g is lo_g and w >= nleft - DIRECT
+        if direct and not own:
+            other_end = line - d == 0 if side == 0 else line + d == L - 1
+            reach = jnp.logical_or(inner, both(other_end, can))
+        along = both(has, reach)
         across = None
-        if own and (g is lo_g or (d == 1 and w < SHORT)):
+        if own and ((g is lo_g and not (direct and d == L - 1)) or (g is lr_g and d == 1 and w < SHORT)):
             across = both(has, at_end)
         return j, has, along, across
 

time: 89.2 us -> 88.8 us (level)
  no operation moved by 1% of the time
where the time goes in v4:
time: 88.8 us; the launch traced here: 88.6 us
  Pallas kernels  87.3 us (98%)
  local copies, waits for them, and re-layouts  1.32 us (1%)
    pallas_call x1, Pallas kernels, body(): pl.pallas_call(functools.partial(kernel, R, C, chunk, DETOUR), out_shape=...  87.3 us

profile of v4, /device:TPU:1, one launch (start us, length us, event | category | flops | bytes accessed | tf_op | source)
XLA Modules:
  0.0 88.6 jit_solution(2075667458972759100)
XLA Ops:
  0.0 87.3 %shard_map.55 = f32[1024,512]{1,0:T(8,128)S(1)} custom-call(f32[1024,512]{1,0:T(8,128)} %x_in.1, f32[1,128,512]{2,1,0:T(8,128)} %rr_in.1, f32[1,128,512]{2,1,0:T(8,128)} %ro_in.1, f32[2,64,512]{2,1,0:T(8,128)} %lr_in.1, f32[2,64,512]{2,1,0:T(8,128)} %lo_in.1), custom_call_target="tpu_custom_call" | custom-call | tf_op jit(solution)/shard_map/pallas_call | solution.py:446
  87.3 1.3 %copy.7 = f32[1024,512]{1,0:T(8,128)} copy(f32[1024,512]{1,0:T(8,128)S(1)} %shard_map.55) | data formatting | bytes 4194304
